TPU v7x, 256 devices: a whole 4x4x8 slice. The times are simulated.
256 devices in a mesh: grp: 16 (over z_lo, x, core), peak: 16 (over y, z_hi).
Axes of the slice: x: 4, y: 4, z: 8 (z_hi: 4, z_lo: 2; z = z_hi * 2 + z_lo), core: 2. Of those that a mesh axis runs over, the one named last changes fastest.
Arguments:
- counts: bfloat16 [1024, 524288], P(None, ('grp', 'peak')), may hold values from 0.099609375 to 4
- tile_mask: int32 [1024, 4096], P(None, ('grp', 'peak')), may hold values 0 or 1
- neighbours: int32 [1024, 15], P(('grp', 'peak')), may hold values from 0 to 1023, as said below
- peak_weight: bfloat16 [524288, 512], P(('grp', 'peak')), may hold values from -0.013671875 to 0.013671875
- gain: float32 [512], replicated, may hold values from 0.25 to 1.75
- w_in: bfloat16 [512, 512], replicated, may hold values from -0.25 to 0.25
- w_out: bfloat16 [512, 256], replicated, may hold values from -0.25 to 0.25
Outputs:
- peak_grad: float32 [524288, 512], P(('grp', 'peak'))
- gain_grad: float32 [512], replicated
- in_grad: float32 [512, 512], replicated
- out_grad: float32 [512, 256], replicated
Inputs may be any that keep to these rules, and one draw needn't show every extreme that they name: `neighbours`: every entry is a cell index other than its own row's cell.
All inputs are finite; a program needn't handle non-finite values. No bound on the sum of `tile_mask` on one device may be relied on, other than what follows from the above.
Results may differ from a plain program's by a relative error of at most 0.012.
Values may be sent and summed in bfloat16 or wider, within the bound.
A program may use at most 64 MiB of HBM per device.

v0:
```python
import jax
import jax.numpy as jnp
from jax import lax
from jax.sharding import PartitionSpec as P

TILE = 128
K = 15
sharpness_divisor = 0.2
eps_norm = 1e-06
gelu_coef = 0.7978845608
cubic_coef = 0.044715


def gelu_tanh(values):
    return (
        0.5
        * values
        * (1.0 + jnp.tanh(gelu_coef * (values + cubic_coef * values * values * values)))
    )


def gelu_slope(values):
    tangent = jnp.tanh(gelu_coef * (values + cubic_coef * values * values * values))
    return 0.5 * (1.0 + tangent) + 0.5 * values * (1.0 - tangent * tangent) * gelu_coef * (
        1.0 + 3.0 * cubic_coef * values * values
    )


def collapsed_lines(left, right):
    return lax.dot_general(
        left, right, (((0,), (0,)), ((), ())), preferred_element_type=jnp.float32
    )


def tower_forward(hidden, gain, w_in, w_out):
    scale = lax.rsqrt(jnp.mean(hidden * hidden, axis=1, keepdims=True) + eps_norm)
    normed = hidden * scale
    rounded = (normed * gain[None, :]).astype(jnp.bfloat16)
    preact = jnp.dot(rounded, w_in, preferred_element_type=jnp.float32)
    activ = gelu_tanh(preact).astype(jnp.bfloat16)
    project = jnp.dot(activ, w_out, preferred_element_type=jnp.float32)
    length = lax.rsqrt(jnp.sum(project * project, axis=1, keepdims=True) + eps_norm)
    unit = project * length
    return ((scale, normed, rounded, preact, activ, length, unit), unit.astype(jnp.bfloat16))


def tower_backward(vector_derivative, gain, w_in, w_out, saved):
    scale, normed, rounded, preact, activ, length, unit = saved
    dproj = (
        length
        * (vector_derivative - unit * jnp.sum(unit * vector_derivative, axis=1, keepdims=True))
    ).astype(jnp.bfloat16)
    out_grad = collapsed_lines(activ, dproj)
    dact = jnp.dot(dproj, w_out.T, preferred_element_type=jnp.float32)
    dpre = (dact * gelu_slope(preact)).astype(jnp.bfloat16)
    in_grad = collapsed_lines(rounded, dpre)
    dround = jnp.dot(dpre, w_in.T, preferred_element_type=jnp.float32)
    gain_grad = jnp.sum(dround * normed, axis=0)
    dnorm = dround * gain[None, :]
    dhidden = scale * (dnorm - normed * jnp.mean(dnorm * normed, axis=1, keepdims=True))
    return (dhidden.astype(jnp.bfloat16), gain_grad, in_grad, out_grad)


def count_lists(lists, column_ids):
    tallies = jnp.zeros((lists.shape[0], column_ids.shape[1]), jnp.float32)
    for slot in range(lists.shape[1]):
        tallies = tallies + (lists[:, slot][:, None] == column_ids).astype(jnp.float32)
    return tallies


def body(counts, tile_mask, neighbours, peak_weight, gain, w_in, w_out):
    total_cells = counts.shape[0]
    own_rows = neighbours.shape[0]
    position = lax.axis_index(("grp", "peak"))
    first_row = position * own_rows
    masked = counts * jnp.repeat(tile_mask.astype(jnp.bfloat16), TILE, axis=1)
    whole_term = jnp.dot(masked, peak_weight, preferred_element_type=jnp.float32)
    hidden = lax.psum_scatter(whole_term, ("grp", "peak"), scatter_dimension=0, tiled=True)
    saved, sample_vectors = tower_forward(hidden, gain, w_in, w_out)
    codes_whole = lax.all_gather(sample_vectors, ("grp", "peak"), axis=0, tiled=True)
    affinity_scores = (
        jnp.einsum("ce,ke->ck", sample_vectors, codes_whole, preferred_element_type=jnp.float32)
        / sharpness_divisor
    )
    row_ids = lax.broadcasted_iota(jnp.int32, (own_rows, total_cells), 0) + first_row
    col_ids = lax.broadcasted_iota(jnp.int32, (own_rows, total_cells), 1)
    expo = jnp.where(row_ids == col_ids, jnp.float32(0.0), jnp.exp(affinity_scores))
    row_total = jnp.sum(expo, axis=1, keepdims=True)
    prob = expo / row_total
    neighbour_coefficients = (prob - count_lists(neighbours, col_ids) / K).astype(jnp.bfloat16)
    source_portion = jnp.dot(
        neighbour_coefficients, codes_whole, preferred_element_type=jnp.float32
    )
    target_portion = lax.psum_scatter(
        collapsed_lines(neighbour_coefficients, sample_vectors),
        ("grp", "peak"),
        scatter_dimension=0,
        tiled=True,
    )
    vector_derivative = (source_portion + target_portion) / sharpness_divisor
    dhidden, gain_part, in_part, out_part = tower_backward(
        vector_derivative, gain, w_in, w_out, saved
    )
    gain_grad, in_grad, out_grad = lax.psum((gain_part, in_part, out_part), ("grp", "peak"))
    dhidden_whole = lax.all_gather(dhidden, ("grp", "peak"), axis=0, tiled=True)
    peak_grad = collapsed_lines(masked, dhidden_whole)
    return (peak_grad, gain_grad, in_grad, out_grad)


def solution(mesh):
    placed = (
        P(None, ("grp", "peak")),
        P(None, ("grp", "peak")),
        P(("grp", "peak"), None),
        P(("grp", "peak"), None),
        P(),
        P(),
        P(),
    )
    return jax.shard_map(
        body,
        mesh=mesh,
        in_specs=placed,
        out_specs=(P(("grp", "peak"), None), P(), P(), P()),
        check_vma=False,
    )
```

profile of v0, /device:TPU:2, one launch (start us, length us, event | category | flops | bytes accessed | tf_op | source)
XLA Modules:
  0.0 2083.6 jit_solution(7782951324887230128)
XLA Ops:
  7.2 0.0 copy-start
  7.2 0.0 all-reduce.7.cloned.1.call-start
  7.2 1.0 convert_element_type.69
  8.2 0.2 copy.12
  8.4 0.0 copy-start.6
  8.4 4.5 broadcast_in_dim.6
  12.9 0.0 copy-start.1
  12.9 1.9 copy-done.1
  14.8 0.0 copy-done
  14.8 0.0 copy-done.6
  14.8 0.0 copy-start.3
  14.8 0.0 copy-start.2
  14.8 0.0 copy-start.5
  14.8 0.0 copy-start.4
  14.8 3.7 fusion.5
  18.5 0.0 all-reduce.7.cloned.1.call-update
  18.5 0.0 all-reduce.9.cloned.1.call-start
  18.6 0.0 copy-done.3
  18.6 0.4 slice_reduce_fusion.14
  19.0 263.9 %all-reduce.7.cloned.1.call-done = f32[1024,512]{1,0:T(8,128)} async-done(((f32[1024,512]{1,0:T(8,128)}), f32[1024,512]{1,0:T(8,128)}) %all-reduce.7.cloned.1.call-update) | async-done | bytes 2097168
  282.9 0.8 multiply_reduce_fusion.2
  283.8 0.0 copy-done.2
  283.8 0.0 copy-done.5
  283.8 0.9 fusion.14
  284.7 0.0 copy-done.4
  284.7 0.3 multiply_reduce_fusion.4
  285.0 0.1 fusion.33
  285.1 603.9 %all-gather = bf16[256,4,256]{2,1,0:T(4,128)(2,1)S(1)} all-gather(bf16[1,4,256]{2,1,0:T(4,128)(2,1)S(1)} %fusion.33), channel_id=1, replica_groups=mesh['grp'=16,'peak'=16] {'grp','peak'}, dimensions={0}, use_global_device_ids=true | all-gather | bytes 526336 | tf_op jit(solution)/shard_map/all_gather | solution.py:80
  889.0 0.9 reshape.34
  889.9 1.4 fusion.20
  891.3 1.4 fusion.17
  892.7 0.0 all-reduce.9.cloned.1.call-update
  892.8 0.0 all-gather.4.cloned.1.call-start
  892.8 385.1 %all-reduce.9.cloned.1.call-done = f32[1024,256]{1,0:T(8,128)} async-done(((f32[1024,256]{1,0:T(8,128)}), f32[1024,256]{1,0:T(8,128)}) %all-reduce.9.cloned.1.call-update) | async-done | bytes 1048592
  1278.0 1.4 multiply_reduce_fusion.3
  1279.4 0.2 fusion.2
  1279.6 1.1 multiply_reduce_fusion
  1280.7 1.4 fusion.12
  1282.1 0.0 all-gather.4.cloned.1.call-update
  1282.1 0.0 all-reduce.11.cloned.1.call-start
  1282.1 75.4 %psum.21 = f32[512]{0:T(512)} all-reduce(f32[512]{0:T(512)S(1)} %get-tuple-element.4), channel_id=1, replica_groups=mesh['grp'=16,'peak'=16] {'grp','peak'}, use_global_device_ids=true, to_apply=%region_8.9 | all-reduce | flops 512 | bytes 4096 | tf_op jit(solution)/shard_map/psum | solution.py:104
  1357.6 1.1 fusion.15
  1358.7 2.1 fusion.13
  1360.8 0.0 all-reduce.11.cloned.1.call-update
  1360.8 449.7 %all-gather.4.cloned.1.call-done = bf16[256,4,512]{2,1,0:T(4,128)(2,1)} async-done(((bf16[1,4,512]{2,1,0:T(4,128)(2,1)}), bf16[256,4,512]{2,1,0:T(4,128)(2,1)}) %all-gather.4.cloned.1.call-update) | async-done | bytes 1048592 | tf_op jit(solution)/shard_map/all_gather | solution.py:105
  1810.4 1.3 reshape.36
  1811.8 8.1 fusion.4
  1819.9 253.0 %all-reduce.11.cloned.1.call-done = (f32[512,512]{1,0:T(8,128)}, f32[512,256]{1,0:T(8,128)}) async-done(((f32[512,512]{1,0:T(8,128)}, f32[512,256]{1,0:T(8,128)}), (f32[512,512]{1,0:T(8,128)}, f32[512,256]{1,0:T(8,128)})) %all-reduce.11.cloned.1.call-update) | async-done | bytes 1572880 | tf_op jit(solution)/shard_map/psum | solution.py:104
  2072.9 2.3 copy.21
  2075.2 1.9 copy.22
  (4 shorter events, 0.0 us)
Async XLA Ops:
  7.2 7.6 copy-start
  7.2 275.7 %all-reduce.7.cloned.1.call-start = ((), (), s32[]{:S(2)}) async-start(), calls=%async_computation.1 | async-start | bytes 4194304
  8.4 6.4 copy-start.6
  12.9 1.9 copy-start.1
  14.8 3.8 copy-start.3
  14.8 269.0 %copy-start.2 = (bf16[512,512]{1,0:T(8,128)(2,1)S(1)}, bf16[512,512]{1,0:T(8,128)(2,1)}, u32[]{:S(2)}) copy-start(bf16[512,512]{1,0:T(8,128)(2,1)} %param.12) | copy-start | bytes 1572868
  14.8 269.0 %copy-start.5 = (f32[512]{0:T(512)S(1)}, f32[512]{0:T(512)}, u32[]{:S(2)}) copy-start(f32[512]{0:T(512)} %param.11) | copy-start | bytes 6148
  14.8 269.9 %copy-start.4 = (bf16[512,256]{1,0:T(8,128)(2,1)S(1)}, bf16[512,256]{1,0:T(8,128)(2,1)}, u32[]{:S(2)}) copy-start(bf16[512,256]{1,0:T(8,128)(2,1)} %param.13) | copy-start | bytes 786436
  18.5 1259.4 %all-reduce.9.cloned.1.call-start = ((), (), s32[]{:S(2)}) async-start(), calls=%async_computation.2 | async-start | bytes 2097152
  892.8 917.7 %all-gather.4.cloned.1.call-start = ((), (), s32[]{:S(2)}) async-start(), calls=%async_computation | async-start | bytes 1052672 | tf_op jit(solution)/shard_map/all_gather | solution.py:105
  1282.1 790.9 %all-reduce.11.cloned.1.call-start = ((), (), s32[]{:S(2)}) async-start(), calls=%async_computation.3 | async-start | bytes 3145728 | tf_op jit(solution)/shard_map/psum | solution.py:104
Sparse Core Ops, SparseCore 0:
  18.6 264.2 all-reduce.6
  892.9 385.0 all-reduce.8
  1282.2 528.1 all-gather.3
  1817.2 255.7 all-reduce.10
where the time goes:
time: 2080 us
  waiting for transfers between devices  1350 us (65%)
  blocking collectives  679 us (33%)
  matrix products  21.7 us (1%)
    unnamed x6, waiting for transfers between devices  649 us
    all_gather x1, blocking collectives, body(): lax.all_gather(sample_vectors, ('grp', 'peak'), axis=0, tiled=True)  604 us
    all_gather x1, waiting for transfers between devices, body(): dhidden_whole = lax.all_gather(dhidden, ('grp', 'peak'), axis=0, tiled=True)  450 us
    psum x1, waiting for transfers between devices, body(): lax.psum((gain_part, in_part, out_part), ('grp', 'peak'))  253 us
    psum x1, blocking collectives, body(): lax.psum((gain_part, in_part, out_part), ('grp', 'peak'))  75.4 us
  transfers between devices with their start and end apart: 4, of which 4 were waited for; matrix products, arithmetic and copies ran while one was open for 1% of the time, Pallas kernels for 0%

commit v1 on v0

--- a/solution.py
+++ b/solution.py
@@ -77,7 +77,12 @@
     whole_term = jnp.dot(masked, peak_weight, preferred_element_type=jnp.float32)
     hidden = lax.psum_scatter(whole_term, ("grp", "peak"), scatter_dimension=0, tiled=True)
     saved, sample_vectors = tower_forward(hidden, gain, w_in, w_out)
-    codes_whole = lax.all_gather(sample_vectors, ("grp", "peak"), axis=0, tiled=True)
+    codes_whole = jnp.concatenate(
+        lax.all_to_all(
+            jnp.stack([sample_vectors] * lax.axis_size(("grp", "peak"))), ("grp", "peak"), 0, 0
+        ),
+        axis=0,
+    )
     affinity_scores = (
         jnp.einsum("ce,ke->ck", sample_vectors, codes_whole, preferred_element_type=jnp.float32)
         / sharpness_divisor

time: 2080 us -> 1380 us (0.66)
  blocking collectives: 679 us -> 75.4 us
  waiting for transfers between devices: 1350 us -> 1240 us
    all_gather x1 -> x0, blocking collectives: 604 us -> none  [body(): lax.all_gather(sample_vectors, ('grp', 'peak'), axis=0, tiled=True)]
    unnamed x6, waiting for transfers between devices: 649 us -> 515 us
  transfers between devices with their start and end apart: 4 -> 5, of which waited for: 4 -> 5; matrix products, arithmetic and copies ran while one was open for 1% -> 1% of each run, Pallas kernels for 0% -> 0%
where the time goes in v1:
time: 1380 us
  waiting for transfers between devices  1240 us (90%)
  blocking collectives  75.4 us (5%)
  matrix products  21.7 us (2%)
  local copies, waits for them, and re-layouts  14.3 us (1%)
  between operations  13.9 us (1%)
    unnamed x6, waiting for transfers between devices  515 us
    all_gather x1, waiting for transfers between devices, body(): dhidden_whole = lax.all_gather(dhidden, ('grp', 'peak'), axis=0, tiled=True)  450 us
    psum x1, waiting for transfers between devices, body(): lax.psum((gain_part, in_part, out_part), ('grp', 'peak'))  253 us
    psum x1, blocking collectives, body(): lax.psum((gain_part, in_part, out_part), ('grp', 'peak'))  75.4 us
  transfers between devices with their start and end apart: 5, of which 5 were waited for; matrix products, arithmetic and copies ran while one was open for 1% of the time, Pallas kernels for 0%

profile of v1, /device:TPU:2, one launch (start us, length us, event | category | flops | bytes accessed | tf_op | source)
XLA Modules:
  0.0 1375.8 jit_solution(15516730377406292002)
XLA Ops:
  7.2 0.0 copy-start
  7.2 0.0 all-reduce.7.cloned.1.call-start
  7.2 1.0 convert_element_type.69
  8.2 0.2 copy.12
  8.4 0.0 copy-start.6
  8.4 4.5 broadcast_in_dim.6
  12.9 0.0 copy-start.1
  12.9 1.9 copy-done.1
  14.8 0.0 copy-done
  14.8 0.0 copy-done.6
  14.8 0.0 copy-start.2
  14.8 0.0 copy-start.5
  14.8 0.0 copy-start.4
  14.8 3.7 fusion.5
  18.5 0.0 copy-start.3
  18.5 0.0 all-reduce.7.cloned.1.call-update
  18.5 264.4 %all-reduce.7.cloned.1.call-done = f32[1024,512]{1,0:T(8,128)} async-done(((f32[1024,512]{1,0:T(8,128)}), f32[1024,512]{1,0:T(8,128)}) %all-reduce.7.cloned.1.call-update) | async-done | bytes 2097168
  282.9 0.8 multiply_reduce_fusion.2
  283.8 0.0 copy-done.2
  283.8 0.0 copy-done.5
  283.8 0.9 fusion.14
  284.7 0.0 copy-done.4
  284.7 0.3 multiply_reduce_fusion.4
  285.0 0.1 multiply_convert_fusion.4
  285.1 0.9 stack.2
  286.0 10.4 all-to-all-start
  296.4 0.0 all-reduce.9.cloned.1.call-start
  296.5 0.0 copy-done.3
  296.5 0.4 slice_reduce_fusion.14
  296.9 19.3 %all-to-all-done = bf16[256,4,256]{2,1,0:T(4,128)(2,1)S(1)} async-done(((bf16[256,4,256]{2,1,0:T(4,128)(2,1)}), bf16[256,4,256]{2,1,0:T(4,128)(2,1)S(1)}, u32[]{:S(2)}, u32[]{:S(2)}) %all-to-all-start) | async-done | bytes 524320 | tf_op jit(solution)/shard_map/all_to_all | solution.py:81
  316.2 0.9 reshape.38
  317.2 1.4 fusion.20
  318.6 1.4 fusion.17
  320.0 0.0 all-reduce.9.cloned.1.call-update
  320.0 0.0 all-gather.3.cloned.1.call-start
  320.1 250.2 %all-reduce.9.cloned.1.call-done = f32[1024,256]{1,0:T(8,128)} async-done(((f32[1024,256]{1,0:T(8,128)}), f32[1024,256]{1,0:T(8,128)}) %all-reduce.9.cloned.1.call-update) | async-done | bytes 1048592
  570.3 1.4 multiply_reduce_fusion.3
  571.7 0.2 fusion.2
  571.9 1.1 multiply_reduce_fusion
  573.0 1.4 fusion.12
  574.4 0.0 all-gather.3.cloned.1.call-update
  574.4 0.0 all-reduce.11.cloned.1.call-start
  574.5 75.4 %psum.21 = f32[512]{0:T(512)} all-reduce(f32[512]{0:T(512)S(1)} %get-tuple-element.4), channel_id=1, replica_groups=mesh['grp'=16,'peak'=16] {'grp','peak'}, use_global_device_ids=true, to_apply=%region_8.9 | all-reduce | flops 512 | bytes 4096 | tf_op jit(solution)/shard_map/psum | solution.py:109
  649.9 1.1 fusion.15
  651.0 2.1 fusion.13
  653.1 0.0 all-reduce.11.cloned.1.call-update
  653.1 449.7 %all-gather.3.cloned.1.call-done = bf16[256,4,512]{2,1,0:T(4,128)(2,1)} async-done(((bf16[1,4,512]{2,1,0:T(4,128)(2,1)}), bf16[256,4,512]{2,1,0:T(4,128)(2,1)}) %all-gather.3.cloned.1.call-update) | async-done | bytes 1048592 | tf_op jit(solution)/shard_map/all_gather | solution.py:110
  1102.8 1.3 reshape.40
  1104.1 8.1 fusion.4
  1112.2 252.9 %all-reduce.11.cloned.1.call-done = (f32[512,512]{1,0:T(8,128)}, f32[512,256]{1,0:T(8,128)}) async-done(((f32[512,512]{1,0:T(8,128)}, f32[512,256]{1,0:T(8,128)}), (f32[512,512]{1,0:T(8,128)}, f32[512,256]{1,0:T(8,128)})) %all-reduce.11.cloned.1.call-update) | async-done | bytes 1572880 | tf_op jit(solution)/shard_map/psum | solution.py:109
  1365.1 2.3 copy.21
  1367.4 1.9 copy.22
  (4 shorter events, 0.0 us)
Async XLA Ops:
  7.2 7.6 copy-start
  7.2 275.8 %all-reduce.7.cloned.1.call-start = ((), (), s32[]{:S(2)}) async-start(), calls=%async_computation.2 | async-start | bytes 4194304
  8.4 6.4 copy-start.6
  12.9 1.9 copy-start.1
  14.8 269.0 %copy-start.2 = (bf16[512,512]{1,0:T(8,128)(2,1)S(1)}, bf16[512,512]{1,0:T(8,128)(2,1)}, u32[]{:S(2)}) copy-start(bf16[512,512]{1,0:T(8,128)(2,1)} %param.12) | copy-start | bytes 1572868
  14.8 269.0 %copy-start.5 = (f32[512]{0:T(512)S(1)}, f32[512]{0:T(512)}, u32[]{:S(2)}) copy-start(f32[512]{0:T(512)} %param.11) | copy-start | bytes 6148
  14.8 269.9 %copy-start.4 = (bf16[512,256]{1,0:T(8,128)(2,1)S(1)}, bf16[512,256]{1,0:T(8,128)(2,1)}, u32[]{:S(2)}) copy-start(bf16[512,256]{1,0:T(8,128)(2,1)} %param.13) | copy-start | bytes 786436
  18.5 278.0 %copy-start.3 = (s32[4,15]{1,0:T(4,128)S(1)}, s32[4,15]{1,0:T(4,128)}, u32[]{:S(2)}) copy-start(s32[4,15]{1,0:T(4,128)} %param.9) | copy-start | bytes 724
  286.0 30.2 %all-to-all-start = ((bf16[256,4,256]{2,1,0:T(4,128)(2,1)}), bf16[256,4,256]{2,1,0:T(4,128)(2,1)S(1)}, u32[]{:S(2)}, u32[]{:S(2)}) async-start(bf16[256,4,256]{2,1,0:T(4,128)(2,1)} %stack.2), calls=%async_computation | async-start | bytes 1048576 | tf_op jit(solution)/shard_map/all_to_all | solution.py:81
  296.4 273.9 %all-reduce.9.cloned.1.call-start = ((), (), s32[]{:S(2)}) async-start(), calls=%async_computation.3 | async-start | bytes 2097152
  320.0 782.8 %all-gather.3.cloned.1.call-start = ((), (), s32[]{:S(2)}) async-start(), calls=%async_computation.1 | async-start | bytes 1052672 | tf_op jit(solution)/shard_map/all_gather | solution.py:110
  574.4 790.7 %all-reduce.11.cloned.1.call-start = ((), (), s32[]{:S(2)}) async-start(), calls=%async_computation.4 | async-start | bytes 3145728 | tf_op jit(solution)/shard_map/psum | solution.py:109
Sparse Core Ops, SparseCore 0:
  18.6 264.2 all-reduce.6
  320.1 250.1 all-reduce.8
  574.5 528.1 all-gather.2
  1109.5 255.5 all-reduce.10
